TPU v7x, 32 devices: a whole 2x2x4 slice. The times are simulated.
32 devices in a mesh: rows: 8 (over y, x, core), feat: 4 (over z).
Axes of the slice: x: 2, y: 2, z: 4, core: 2. Of those that a mesh axis runs over, the one named last changes fastest.
Arguments:
- queries: bfloat16 [49152, 4096], P('rows', 'feat'), may hold values from -6 to 6
- projection: bfloat16 [4096, 128], P('feat'), may hold values from -0.09375 to 0.09375
- models: float32 [64, 128], replicated, may hold values from -0.5 to 0.5
- first: int32 [49152], P('rows'), may hold values from 0 to 63
- second: int32 [49152], P('rows'), may hold values from 0 to 63
- wins: int32 [49152], P('rows'), may hold values 0 or 1
Outputs:
- update_proj: float32 [4096, 128], P('feat')
- update_models: float32 [64, 128], replicated
- loss: float32 [], replicated
All inputs are finite; a program needn't handle non-finite values. No bound on the sum of `wins` on one device may be relied on, other than what follows from the above.
Results may differ from a plain program's by a relative error of at most 0.00045.
The roundings to bfloat16 on the way count: a program that leaves them out, or rounds other values in their place, can miss the bound.
Values may be sent and summed in bfloat16 or wider, within the bound.
A program may use at most 64 MiB of HBM per device.

v0:
```python
import jax
import jax.numpy as jnp
from jax import lax
from jax.sharding import PartitionSpec as P

D = 4096
R = 128
NM = 64


def pair_gap(models, first, second):
    return jnp.take(models, first, axis=0) - jnp.take(models, second, axis=0)


def pick_table(models, first, second):
    labels = jnp.arange(models.shape[0], dtype=jnp.int32)[:, None]
    return (labels == first[None, :]).astype(jnp.float32) - (labels == second[None, :]).astype(
        jnp.float32
    )


def body(queries, projection, models, first, second, wins):
    local_rows = queries.shape[0]
    total_rows = float(local_rows * lax.axis_size("rows"))
    partial_value = jnp.dot(queries, projection, preferred_element_type=jnp.float32)
    gap = pair_gap(models, first, second)
    margin = lax.psum(jnp.sum(partial_value * gap, axis=-1), "feat")
    sign = 2.0 * wins.astype(jnp.float32) - 1.0
    loss_part = jnp.sum(jax.nn.softplus(-sign * margin)) / total_rows
    coef = -sign * jax.nn.sigmoid(-sign * margin) / total_rows
    back = (coef[:, None] * gap).astype(jnp.bfloat16)
    pick = pick_table(models, first, second)
    model_part = jnp.dot(pick, coef[:, None] * partial_value, precision=lax.Precision.HIGHEST)
    feat_count = float(lax.axis_size("feat"))
    grad_models, loss = lax.psum((model_part, loss_part / feat_count), ("rows", "feat"))
    model_square = jnp.sum(grad_models * grad_models)
    entries = jnp.sqrt(jnp.float32(D * R + NM * R))
    grad_local = jnp.dot(queries.T, back, preferred_element_type=jnp.float32)
    grad_proj = lax.psum(grad_local, "rows")
    square = lax.psum(jnp.sum(grad_proj * grad_proj), "feat")
    scale = entries / (jnp.sqrt(square + model_square) + 1e-06)
    update_proj = scale * grad_proj
    return (update_proj, scale * grad_models, loss)


def solution(mesh):
    in_specs = (P("rows", "feat"), P("feat", None), P(), P("rows"), P("rows"), P("rows"))
    out_specs = (P("feat", None), P(), P())
    return jax.shard_map(body, mesh=mesh, in_specs=in_specs, out_specs=out_specs, check_vma=False)
```

profile of v0, /device:TPU:0, one launch (start us, length us, event | category | flops | bytes accessed | tf_op | source)
XLA Modules:
  0.0 177.5 jit_solution(17190203566094224995)
XLA Ops:
  7.2 0.0 copy-start
  7.2 0.0 all-reduce.3.cloned.1.call-start
  7.2 0.7 fusion.14
  8.0 0.8 compare_and_fusion
  8.8 0.7 fusion.13
  9.5 20.9 %gather_fusion.1 = f32[6144,128]{1,0:T(8,128)} fusion(f32[64,128]{1,0:T(8,128)S(1)} %copy-done.1, s32[6144]{0:T(1024)S(1)} %fusion.14), kind=kCustom, calls=%fused_computation.1.clone | custom fusion | bytes 6316032 | tf_op jit(solution)/shard_map/jit(_take)/gather | solution.py:12
  30.4 2.4 %copy.10 = f32[6144,128]{0,1:T(8,128)S(1)} copy(f32[6144,128]{1,0:T(8,128)} %gather_fusion.1) | data formatting | bytes 6291456 | tf_op jit(solution)/shard_map/jit(_take)/gather | solution.py:12
  32.8 20.9 %gather_fusion = f32[6144,128]{1,0:T(8,128)} fusion(f32[64,128]{1,0:T(8,128)S(1)} %copy-done.1, s32[6144]{0:T(1024)S(1)} %fusion.13), kind=kCustom, calls=%fused_computation.clone | custom fusion | bytes 6316032 | tf_op jit(solution)/shard_map/jit(_take)/gather | solution.py:12
  53.7 3.5 %copy.9 = f32[6144,128]{0,1:T(8,128)} copy(f32[6144,128]{1,0:T(8,128)} %gather_fusion) | data formatting | bytes 6291456 | tf_op jit(solution)/shard_map/jit(_take)/gather | solution.py:12
  57.2 11.7 %multiply_reduce_fusion = (f32[6144]{0:T(1024)S(1)}, f32[6144,128]{0,1:T(8,128)}) fusion(f32[6144,128]{0,1:T(8,128)S(1)} %copy.10, pred[6144]{0:T(1024)(128)(4,1)S(1)} %get-tuple-element.13, f32[6144,128]{0,1:T(8,128)} %copy.9, pred[6144]{0:T(1024)(128)(4,1)S(1)} %get-tuple-element.14, bf16[6144,1024]{1,0:T(8,128)(2,1)} %param.8, ...), kind=kOutput, calls=%fused_computation.6 | convolution fusion | flops 1614538752 | bytes 22319104 | tf_op jit(solution)/shard_map/dot_general | solution.py:25
  68.9 20.8 %psum.35 = f32[6144]{0:T(1024)S(1)} all-reduce(f32[6144]{0:T(1024)S(1)} %get-tuple-element.11), channel_id=1, replica_groups=mesh['rows'=8,'feat'=4] {'feat'}, use_global_device_ids=true, to_apply=%region_1.3 | all-reduce | flops 6144 | bytes 49152 | tf_op jit(solution)/shard_map/psum | solution.py:27
  89.6 0.0 copy-done.4
  89.6 0.6 fusion.11
  90.3 8.3 %fusion.8 = f32[1024,128]{0,1:T(8,128)} fusion(bf16[6144,1024]{1,0:T(8,128)(2,1)} %param.8, f32[6144]{0:T(1024)S(1)} %get-tuple-element.10, f32[6144,128]{0,1:T(8,128)S(1)} %copy.10, f32[6144,128]{0,1:T(8,128)} %copy.9, pred[6144]{0:T(1024)(128)(4,1)S(1)} %get-tuple-element.13, pred[6144]{0:T(1024)(128)(4,1)S(1)} %get-tuple-element.14), kind=kOutput, calls=%fused_computation.15 | convolution fusion | flops 1614544896 | bytes 19435520 | tf_op jit(solution)/shard_map/dot_general | solution.py:38
  98.6 0.0 all-reduce.3.cloned.1.call-update
  99.3 5.2 %fusion = f32[64,128]{1,0:T(8,128)S(1)} fusion(f32[6144,128]{0,1:T(8,128)} %get-tuple-element.12, f32[6144]{0:T(1024)S(1)} %get-tuple-element.10, s32[6144]{0:T(1024)S(1)} %copy-done.2, s32[6144]{0:T(1024)S(1)} %copy-done.3), kind=kOutput, calls=%fused_computation.3 | convolution fusion | flops 606732288 | bytes 3252224 | tf_op jit(solution)/shard_map/dot_general | solution.py:33
  104.4 38.9 %all-reduce = (f32[64,128]{1,0:T(8,128)S(1)}, f32[]{:T(128)}) all-reduce(f32[64,128]{1,0:T(8,128)S(1)} %fusion, f32[]{:T(128)S(6)} %div.20), channel_id=1, replica_groups=mesh['rows'=8,'feat'=4] {'rows','feat'}, use_global_device_ids=true, to_apply=%region_5.7 | all-reduce | flops 8193 | bytes 65544 | tf_op jit(solution)/shard_map/psum | solution.py:35
  143.3 8.6 %all-reduce.3.cloned.1.call-done = f32[1024,128]{0,1:T(8,128)} async-done(((f32[1024,128]{0,1:T(8,128)}), f32[1024,128]{0,1:T(8,128)}) %all-reduce.3.cloned.1.call-update) | async-done | bytes 524304 | tf_op jit(solution)/shard_map/psum | solution.py:39
  151.9 1.8 %multiply_reduce_fusion.1 = f32[]{:T(128)} fusion(f32[1024,128]{0,1:T(8,128)} %all-reduce.3.cloned.1.call-done), kind=kLoop, calls=%fused_computation.18 | loop fusion | flops 262143 | bytes 524292 | tf_op jit(solution)/shard_map/reduce_sum | solution.py:40
  153.7 0.6 multiply_reduce_fusion.2
  154.3 12.2 %psum.37 = f32[]{:T(128)} all-reduce(f32[]{:T(128)} %multiply_reduce_fusion.1), channel_id=1, replica_groups=mesh['rows'=8,'feat'=4] {'feat'}, use_global_device_ids=true, to_apply=%region_4.6 | all-reduce | flops 1 | bytes 8 | tf_op jit(solution)/shard_map/psum | solution.py:40
  168.0 0.6 broadcast_multiply_fusion.1
  168.6 1.1 broadcast_multiply_fusion
  169.7 1.0 copy.11
  (8 shorter events, 0.0 us)
Async XLA Ops:
  7.2 50.0 %copy-start = (bf16[1024,128]{1,0:T(8,128)(2,1)S(1)}, bf16[1024,128]{1,0:T(8,128)(2,1)}, u32[]{:S(2)}) copy-start(bf16[1024,128]{1,0:T(8,128)(2,1)} %param.9) | copy-start | bytes 786436
  7.2 2.3 %copy-start.1 = (f32[64,128]{1,0:T(8,128)S(1)}, f32[64,128]{1,0:T(8,128)}, u32[]{:S(2)}) copy-start(f32[64,128]{1,0:T(8,128)} %param.10) | copy-start | bytes 98308
  7.2 144.8 %all-reduce.3.cloned.1.call-start = ((), (), s32[]{:S(2)}) async-start(), calls=%async_computation | async-start | bytes 1048576 | tf_op jit(solution)/shard_map/psum | solution.py:39
  57.2 32.4 %copy-start.4 = (s32[6144]{0:T(1024)S(1)}, s32[6144]{0:T(1024)}, u32[]{:S(2)}) copy-start(s32[6144]{0:T(1024)} %param.13) | copy-start | bytes 73732
  90.3 9.0 %copy-start.2 = (s32[6144]{0:T(1024)S(1)}, s32[6144]{0:T(1024)}, u32[]{:S(2)}) copy-start(s32[6144]{0:T(1024)} %param.12) | copy-start | bytes 73732
  90.3 9.0 %copy-start.3 = (s32[6144]{0:T(1024)S(1)}, s32[6144]{0:T(1024)}, u32[]{:S(2)}) copy-start(s32[6144]{0:T(1024)} %param.11) | copy-start | bytes 73732
Sparse Core Ops, SparseCore 0:
  98.7 53.1 all-reduce.2
where the time goes:
time: 178 us
  blocking collectives  71.9 us (40%)
  local copies, waits for them, and re-layouts  48.7 us (27%)
  matrix products  25.2 us (14%)
  between operations  16.1 us (9%)
  waiting for transfers between devices  8.62 us (5%)
  other arithmetic  6.98 us (4%)
    gather x4, local copies, waits for them, and re-layouts, pair_gap(): return jnp.take(models, first, axis=0) - jnp.take(models, second, axis=0)  47.7 us
    psum x1, blocking collectives, body(): lax.psum((model_part, loss_part / feat_count), ('rows', 'feat'))  38.9 us
    psum x1, blocking collectives, body(): margin = lax.psum(jnp.sum(partial_value * gap, axis=-1), 'feat')  20.8 us
    psum x1, blocking collectives, body(): square = lax.psum(jnp.sum(grad_proj * grad_proj), 'feat')  12.2 us
    dot_general x1, matrix products, body(): jnp.dot(queries, projection, preferred_element_type=jnp.float32)  11.7 us
    psum x1, waiting for transfers between devices, body(): grad_proj = lax.psum(grad_local, 'rows')  8.61 us
    dot_general x1, matrix products, body(): grad_local = jnp.dot(queries.T, back, preferred_element_type=jnp.float32)  8.29 us
    dot_general x1, matrix products, body(): jnp.dot(pick, coef[:, None] * partial_value, precision=lax.Precision.HIGH...  5.18 us
  transfers between devices with their start and end apart: 1, of which 1 were waited for; matrix products, arithmetic and copies ran while one was open for 3% of the time, Pallas kernels for 0%

commit v1 on v0

v1 whole, which is shorter than its diff:
```python
import functools

import jax
import jax.numpy as jnp
from jax import lax
from jax.experimental import pallas as pl
from jax.experimental.pallas import tpu as pltpu
from jax.sharding import PartitionSpec as P

F32 = jnp.float32
BF16 = jnp.bfloat16
SUB = 256
MESH = pl.DeviceIdType.MESH
NT = (((1,), (1,)), ((), ()))


def dot_nt(a, b):
    return lax.dot_general(a, b, NT, preferred_element_type=F32)


def split3(x):
    hi = x.astype(BF16)
    rest = x - hi.astype(F32)
    mid = rest.astype(BF16)
    lo = (rest - mid.astype(F32)).astype(BF16)
    return hi, mid, lo


def kernel(
    nrows, nfeat, chunks, blocks, total_dim,
    q_hbm, proj_ref, models_ref, first_ref, second_ref, wins_ref,
    out_ref, um_ref, loss_ref,
    qv, gap_v, routed_v, back_v, pick_v, marg, gblk, prt, csum, rbuf, gfull,
    mbuf, mprt, mrow, mfeat, mtot, sqf, sqr,
    q_sem, mg_s, mg_r, pr_s, pr_r, rs_s, rs_r, ag_s, ag_r, fw_s, fw_r,
    ma_s, ma_r, mb_s, mb_r, mc_s, mc_r, md_s, md_r, sf_s, sf_r, sr_s, sr_r,
):
    row = lax.axis_index("rows")
    feat = lax.axis_index("feat")
    core = lax.rem(row, 2)
    chip = lax.div(row, 2)
    chips = nrows // 2
    partner = chip * 2 + (1 - core)
    tokens, dloc = qv.shape
    rdim = proj_ref.shape[1]
    nm = models_ref.shape[0]
    t = tokens // chunks
    bw = dloc // blocks
    half = bw // 2
    fs = dloc // nrows
    gpb = half // fs
    mh = mbuf.shape[0] // 2
    total_rows = float(tokens * nrows)

    def qcopy(c):
        at = pl.ds(c * t, t)
        return pltpu.make_async_copy(q_hbm.at[at], qv.at[at], q_sem.at[c])

    for c in range(chunks):
        qcopy(c).start()

    barrier = pltpu.get_barrier_semaphore()
    for d in range(1, nfeat):
        pl.semaphore_signal(
            barrier, inc=1, device_id=(row, lax.rem(feat + d, nfeat)), device_id_type=MESH
        )
    for d in range(1, nrows):
        pl.semaphore_signal(
            barrier, inc=1, device_id=(lax.rem(row + d, nrows), feat), device_id_type=MESH
        )

    def remote(src, dst, send, recv, to_row, to_feat):
        return pltpu.make_async_remote_copy(
            src_ref=src, dst_ref=dst, send_sem=send, recv_sem=recv,
            device_id=(to_row, to_feat), device_id_type=MESH,
        )

    sent = []

    def push(*args):
        cp = remote(*args)
        cp.start()
        sent.append(cp)

    def arrived(dst, send, recv):
        remote(dst, dst, send, recv, partner, feat).wait_recv()

    eye = (
        lax.broadcasted_iota(jnp.int32, (rdim, rdim), 0)
        == lax.broadcasted_iota(jnp.int32, (rdim, rdim), 1)
    ).astype(F32).astype(BF16)
    proj_t = dot_nt(eye, proj_ref[...]).astype(BF16)
    models3 = jnp.concatenate(split3(models_ref[...]), axis=0)
    models3_t = dot_nt(eye, models3).astype(BF16)

    label = lax.broadcasted_iota(jnp.int32, (nm, SUB), 0)
    for s in range(tokens // SUB):
        at = pl.ds(s * SUB, SUB)
        pick = (
            (label == first_ref[:, at]).astype(F32) - (label == second_ref[:, at]).astype(F32)
        ).astype(BF16)
        pick_v[:, at] = pick
        pick3 = jnp.concatenate([pick, pick, pick], axis=0)
        gap_v[:, at] = jnp.dot(models3_t, pick3, preferred_element_type=F32)

    pl.semaphore_wait(barrier, nfeat - 1 + nrows - 1)

    for c in range(chunks):
        qcopy(c).wait()
        for s in range(t // SUB):
            at = pl.ds(c * t + s * SUB, SUB)
            routed = dot_nt(proj_t, qv[at, :])
            routed_v[:, at] = routed
            marg[feat, c, :, pl.ds(s * SUB, SUB)] = jnp.sum(
                routed * gap_v[:, at], axis=0, keepdims=True
            )
        for d in range(1, nfeat):
            push(
                marg.at[feat, c], marg.at[feat, c], mg_s.at[c, d], mg_r.at[c, feat],
                row, lax.rem(feat + d, nfeat),
            )

    loss_row = jnp.zeros((1, t), F32)
    msum = jnp.zeros((nm, 2 * rdim), F32)
    for c in range(chunks):
        for d in range(1, nfeat):
            frm = lax.rem(feat + d, nfeat)
            arrived(marg.at[frm, c], mg_s.at[c, d], mg_r.at[c, frm])
        at = pl.ds(c * t, t)
        margin = marg[0, c]
        for z in range(1, nfeat):
            margin = margin + marg[z, c]
        sign = 2.0 * wins_ref[:, at].astype(F32) - 1.0
        x = -sign * margin
        loss_row = loss_row + (jnp.maximum(x, 0.0) + jnp.log1p(jnp.exp(-jnp.abs(x))))
        coef = -sign * jax.nn.sigmoid(x) / total_rows
        for s in range(t // SUB):
            sub = pl.ds(c * t + s * SUB, SUB)
            cs = coef[:, s * SUB:(s + 1) * SUB]
            back_v[:, sub] = (cs * gap_v[:, sub]).astype(BF16)
            w = cs * routed_v[:, sub]
            hi = w.astype(BF16)
            lo = (w - hi.astype(F32)).astype(BF16)
            msum = msum + dot_nt(pick_v[:, sub], jnp.concatenate([hi, lo], axis=0))

    mbuf[0:nm, :] = msum[:, :rdim] + msum[:, rdim:]
    lsum = loss_row[:, 0:rdim]
    for i in range(1, t // rdim):
        lsum = lsum + loss_row[:, i * rdim:(i + 1) * rdim]
    tail = mbuf.shape[0] - nm
    mbuf[nm:, :] = jnp.where(
        lax.broadcasted_iota(jnp.int32, (tail, rdim), 0) == 0,
        jnp.broadcast_to(lsum, (tail, rdim)), 0.0,
    )
    push(mbuf.at[pl.ds((1 - core) * mh, mh)], mprt, ma_s, ma_r, partner, feat)

    def block_of(i):
        return lax.rem(lax.div(chip, gpb) + 1 + i, blocks)

    def block_grad(i):
        cols = pl.ds(pl.multiple_of(block_of(i) * bw, 128), bw)
        acc = jnp.zeros((rdim, bw), F32)
        for c in range(chunks):
            at = pl.ds(c * t, t)
            acc = acc + jnp.dot(back_v[:, at], qv[at, cols], preferred_element_type=F32)
        gblk[i] = acc.T
        push(
            gblk.at[i, pl.ds((1 - core) * half, half)], prt.at[i], pr_s.at[i], pr_r.at[i],
            partner, feat,
        )

    kept = []

    def chip_sum(i):
        arrived(prt.at[i], pr_s.at[i], pr_r.at[i])
        csum[i] = gblk[i, pl.ds(core * half, half), :] + prt[i]
        for j in range(gpb):
            to = block_of(i) * gpb + j
            if gpb == 1 and i == blocks - 1:
                rbuf[chip] = csum[i, pl.ds(j * fs, fs), :]
                continue
            cp = remote(
                csum.at[i, pl.ds(j * fs, fs)], rbuf.at[chip], rs_s.at[i, j], rs_r.at[chip],
                to * 2 + core, feat,
            )
            if gpb == 1:
                cp.start()
                sent.append(cp)
            else:
                @pl.when(to != chip)
                def _():
                    cp.start()

                @pl.when(to == chip)
                def _():
                    rbuf[chip] = csum[i, pl.ds(j * fs, fs), :]

                kept.append((to, cp))

    block_grad(0)
    arrived(mprt, ma_s, ma_r)
    mrow[chip] = mbuf[pl.ds(core * mh, mh), :] + mprt[...]
    for d in range(1, chips):
        push(
            mrow.at[chip], mrow.at[chip], mb_s.at[d], mb_r.at[chip],
            lax.rem(chip + d, chips) * 2 + core, feat,
        )
    for i in range(1, blocks):
        block_grad(i)
        chip_sum(i - 1)
    for d in range(1, chips):
        frm = lax.rem(chip + d, chips)
        arrived(mrow.at[frm], mb_s.at[d], mb_r.at[frm])
    mr = mrow[0]
    for i in range(1, chips):
        mr = mr + mrow[i]
    mfeat[feat] = mr
    for d in range(1, nfeat):
        push(
            mfeat.at[feat], mfeat.at[feat], mc_s.at[d], mc_r.at[feat],
            row, lax.rem(feat + d, nfeat),
        )
    chip_sum(blocks - 1)

    def offset(c, k):
        return pl.multiple_of(lax.div(c, gpb) * bw + k * half + lax.rem(c, gpb) * fs, 8)

    def slice_of(c, k):
        return gfull.at[pl.ds(offset(c, k), fs)]

    for d in range(1, chips):
        frm = lax.rem(chip + d, chips)
        arrived(rbuf.at[frm], ag_s.at[d], rs_r.at[frm])
    own = rbuf[0]
    for i in range(1, chips):
        own = own + rbuf[i]
    gfull[pl.ds(offset(chip, core), fs), :] = own
    for d in range(1, chips):
        push(
            slice_of(chip, core), slice_of(chip, core), ag_s.at[d], ag_r.at[chip],
            lax.rem(chip + d, chips) * 2 + core, feat,
        )
    push(
        slice_of(chip, core), slice_of(chip, core), fw_s.at[0], fw_r.at[chip], partner, feat
    )
    square = own * own
    sq = square[0:8]
    for i in range(1, fs // 8):
        sq = sq + square[i * 8:(i + 1) * 8]
    sqf[feat] = sq
    for d in range(1, nfeat):
        push(
            sqf.at[feat], sqf.at[feat], sf_s.at[d], sf_r.at[feat],
            row, lax.rem(feat + d, nfeat),
        )

    for d in range(1, nfeat):
        frm = lax.rem(feat + d, nfeat)
        arrived(mfeat.at[frm], mc_s.at[d], mc_r.at[frm])
    mt = mfeat[0]
    for i in range(1, nfeat):
        mt = mt + mfeat[i]
    mtot[core] = mt
    push(mtot.at[core], mtot.at[core], md_s, md_r.at[core], partner, feat)

    for d in range(1, nfeat):
        frm = lax.rem(feat + d, nfeat)
        arrived(sqf.at[frm], sf_s.at[d], sf_r.at[frm])
    sq = sqf[0]
    for i in range(1, nfeat):
        sq = sq + sqf[i]
    sqr[row] = sq
    for d in range(1, nrows):
        push(
            sqr.at[row], sqr.at[row], sr_s.at[d], sr_r.at[row],
            lax.rem(row + d, nrows), feat,
        )

    for d in range(1, chips):
        frm = lax.rem(chip + d, chips)
        arrived(slice_of(frm, core), ag_s.at[d], ag_r.at[frm])
        push(
            slice_of(frm, core), slice_of(frm, core), fw_s.at[d], fw_r.at[frm], partner, feat
        )

    arrived(mtot.at[1 - core], md_s, md_r.at[1 - core])
    grad_models = jnp.concatenate([mtot[0], mtot[1]], axis=0)
    loss_ref[0, 0] = jnp.sum(grad_models[nm:]) / total_rows / float(nfeat)
    grad_models = grad_models[:nm]
    model_square = jnp.sum(grad_models * grad_models)
    for d in range(1, nrows):
        frm = lax.rem(row + d, nrows)
        arrived(sqr.at[frm], sr_s.at[d], sr_r.at[frm])
    sq = sqr[0]
    for i in range(1, nrows):
        sq = sq + sqr[i]
    total = jnp.sum(sq) + model_square
    entries = jnp.sqrt(jnp.full((1, rdim), float(total_dim * rdim + nm * rdim), F32))
    scale = entries / (jnp.sqrt(jnp.full((1, rdim), total, F32)) + 1e-06)
    um_ref[...] = scale * grad_models
    for d in range(chips):
        frm = lax.rem(chip + d, chips)
        arrived(slice_of(frm, 1 - core), fw_s.at[d], fw_r.at[frm])
    out_ref[...] = scale * gfull[...]

    for cp in sent:
        cp.wait_send()
    for to, cp in kept:
        @pl.when(to != chip)
        def _():
            cp.wait_send()


def body(queries, projection, models, first, second, wins):
    nrows, nfeat = lax.axis_size("rows"), lax.axis_size("feat")
    tokens, dloc = queries.shape
    rdim = projection.shape[1]
    nm = models.shape[0]
    chips = nrows // 2
    fs = dloc // nrows
    bw = max(2 * fs, 128)
    blocks = dloc // bw
    half = bw // 2
    gpb = half // fs
    chunks = tokens // 1024
    t = tokens // chunks
    mh = (nm + 16) // 2
    vmem = pl.BlockSpec(memory_space=pltpu.VMEM)
    dma = pltpu.SemaphoreType.DMA
    out, um, loss = pl.pallas_call(
        functools.partial(kernel, nrows, nfeat, chunks, blocks, dloc * nfeat),
        out_shape=(
            jax.ShapeDtypeStruct((dloc, rdim), F32),
            jax.ShapeDtypeStruct((nm, rdim), F32),
            jax.ShapeDtypeStruct((1, 1), F32),
        ),
        in_specs=[pl.BlockSpec(memory_space=pl.ANY)] + [vmem] * 5,
        out_specs=(vmem, vmem, pl.BlockSpec(memory_space=pltpu.SMEM)),
        scratch_shapes=[
            pltpu.VMEM((tokens, dloc), BF16),
            pltpu.VMEM((rdim, tokens), F32),
            pltpu.VMEM((rdim, tokens), F32),
            pltpu.VMEM((rdim, tokens), BF16),
            pltpu.VMEM((nm, tokens), BF16),
            pltpu.VMEM((nfeat, chunks, 1, t), F32),
            pltpu.VMEM((blocks, bw, rdim), F32),
            pltpu.VMEM((blocks, half, rdim), F32),
            pltpu.VMEM((blocks, half, rdim), F32),
            pltpu.VMEM((chips, fs, rdim), F32),
            pltpu.VMEM((dloc, rdim), F32),
            pltpu.VMEM((2 * mh, rdim), F32),
            pltpu.VMEM((mh, rdim), F32),
            pltpu.VMEM((chips, mh, rdim), F32),
            pltpu.VMEM((nfeat, mh, rdim), F32),
            pltpu.VMEM((2, mh, rdim), F32),
            pltpu.VMEM((nfeat, 8, rdim), F32),
            pltpu.VMEM((nrows, 8, rdim), F32),
            dma((chunks,)),
            dma((chunks, nfeat)), dma((chunks, nfeat)),
            dma((blocks,)), dma((blocks,)),
            dma((blocks, gpb)), dma((chips,)),
            dma((chips,)), dma((chips,)),
            dma((chips,)), dma((chips,)),
            dma, dma,
            dma((chips,)), dma((chips,)),
            dma((nfeat,)), dma((nfeat,)),
            dma, dma((2,)),
            dma((nfeat,)), dma((nfeat,)),
            dma((nrows,)), dma((nrows,)),
        ],
        compiler_params=pltpu.CompilerParams(
            collective_id=0, has_side_effects=True, vmem_limit_bytes=60 << 20
        ),
    )(
        queries, projection, models,
        first.reshape(1, tokens), second.reshape(1, tokens), wins.reshape(1, tokens),
    )
    return out, um, loss[0, 0]


def solution(mesh):
    in_specs = (P("rows", "feat"), P("feat", None), P(), P("rows"), P("rows"), P("rows"))
    out_specs = (P("feat", None), P(), P())
    return jax.shard_map(body, mesh=mesh, in_specs=in_specs, out_specs=out_specs, check_vma=False)
```

time: 178 us -> 38.4 us (0.22)
  blocking collectives: 71.9 us -> 0 us
  local copies, waits for them, and re-layouts: 48.7 us -> 3.24 us
  Pallas kernels: 0 us -> 32.6 us
  matrix products: 25.2 us -> 0 us
  between operations: 16.1 us -> 2.38 us
  waiting for transfers between devices: 8.62 us -> 0 us
  other arithmetic: 6.98 us -> 0 us
    psum x3 -> x0, blocking collectives: 71.9 us -> none  [the longest x1 38.9 us: body(): lax.psum((model_part, loss_part / feat_count), ('rows', 'feat'))]
    gather x4 -> x0, local copies, waits for them, and re-layouts: 47.7 us -> none  [pair_gap(): return jnp.take(models, first, axis=0) - jnp.take(models, second, axis=0)]
    pallas_call x0 -> x1, Pallas kernels: none -> 32.6 us  [body(): pl.pallas_call(functools.partial(kernel, nrows, nfeat, chunks, blocks, dl...]
    dot_general x3 -> x0, matrix products: 25.2 us -> none  [the longest x1 11.7 us: body(): jnp.dot(queries, projection, preferred_element_type=jnp.float32)]
    psum x1 -> x0, waiting for transfers between devices: 8.61 us -> none  [body(): grad_proj = lax.psum(grad_local, 'rows')]
    reduce_sum x3 -> x0, other arithmetic: 3.01 us -> none  [the longest x1 1.78 us: body(): square = lax.psum(jnp.sum(grad_proj * grad_proj), 'feat')]
    unnamed x11 -> x2, local copies, waits for them, and re-layouts: 1.02 us -> 3.24 us
  transfers between devices with their start and end apart: 1 -> 0, of which waited for: 1 -> 0; matrix products, arithmetic and copies ran while one was open for 3% -> 0% of each run, Pallas kernels for 0% -> 0%
where the time goes in v1:
time: 38.4 us; the launch traced here: 38.2 us
  Pallas kernels  32.6 us (85%)
  local copies, waits for them, and re-layouts  3.24 us (8%)
  between operations  2.38 us (6%)
    pallas_call x1, Pallas kernels, body(): pl.pallas_call(functools.partial(kernel, nrows, nfeat, chunks, blocks, dl...  32.6 us
    unnamed x2, local copies, waits for them, and re-layouts  3.24 us

profile of v1, /device:TPU:0, one launch (start us, length us, event | category | flops | bytes accessed | tf_op | source)
XLA Modules:
  0.0 38.2 jit_solution(10933793999708580024)
XLA Ops:
  0.6 32.6 %shard_map.85 = (f32[1024,128]{1,0:T(8,128)}, f32[64,128]{1,0:T(8,128)}, f32[1,1]{1,0:T(1,128)}) custom-call(bf16[6144,1024]{1,0:T(8,128)(2,1)} %q_hbm.1, bf16[1024,128]{1,0:T(8,128)(2,1)} %proj_ref.1, f32[64,128]{1,0:T(8,128)} %models_ref.1, s32[1,6144]{1,0:T(1,128)} %bitcast.4, s32[1,6144]{1,0:T(1,128)} %bitcast.5, s32[1,6144]{1,0:T(1,128)} %bitcast.6), custom_call_target="tpu_custom_call" | custom-call | tf_op jit(solution)/shard_map/pallas_call | solution.py:330
  33.2 1.9 %copy.12 = f32[1024,128]{1,0:T(8,128)} copy(f32[1024,128]{1,0:T(8,128)} %get-tuple-element.12) | data formatting | bytes 1048576
  35.1 1.4 %copy.13 = f32[64,128]{1,0:T(8,128)} copy(f32[64,128]{1,0:T(8,128)} %get-tuple-element.13) | data formatting | bytes 65536

commit v2 on v1

v2 whole, which is shorter than its diff:
```python
import functools

import jax
import jax.numpy as jnp
from jax import lax
from jax.experimental import pallas as pl
from jax.experimental.pallas import tpu as pltpu
from jax.sharding import PartitionSpec as P

F32 = jnp.float32
BF16 = jnp.bfloat16
SUB = 256
MESH = pl.DeviceIdType.MESH
NT = (((1,), (1,)), ((), ()))


def dot_nt(a, b):
    return lax.dot_general(a, b, NT, preferred_element_type=F32)


def split3(x):
    hi = x.astype(BF16)
    rest = x - hi.astype(F32)
    mid = rest.astype(BF16)
    lo = (rest - mid.astype(F32)).astype(BF16)
    return hi, mid, lo


def kernel(
    nrows, nfeat, chunks, blocks, total_dim,
    q_hbm, proj_hbm, models_hbm, first_hbm, second_hbm, wins_hbm,
    out_ref, small_ref,
    qv, proj_ref, models_ref, first_ref, second_ref, wins_ref,
    gap_v, routed_v, back_v, pick_v, marg, acc_v, gblk, prt, csum, rbuf, gfull,
    mbuf, mprt, mrow, mfeat, mtot, sqf, sqr,
    q_sem, in_sem, mg_s, mg_r, pr_s, pr_r, rs_s, rs_r, ag_s, ag_r, fw_s, fw_r,
    ma_s, ma_r, mb_s, mb_r, mc_s, mc_r, md_s, md_r, sf_s, sf_r, sr_s, sr_r,
):
    row = lax.axis_index("rows")
    feat = lax.axis_index("feat")
    core = lax.rem(row, 2)
    chip = lax.div(row, 2)
    chips = nrows // 2
    partner = chip * 2 + (1 - core)
    tokens, dloc = qv.shape
    rdim = proj_ref.shape[1]
    nm = models_ref.shape[0]
    t = tokens // chunks
    early = max(1, chunks * 2 // 3)
    bw = dloc // blocks
    half = bw // 2
    fs = dloc // nrows
    gpb = half // fs
    mh = mbuf.shape[0] // 2
    total_rows = float(tokens * nrows)

    def qcopy(c):
        at = pl.ds(c * t, t)
        return pltpu.make_async_copy(q_hbm.at[at], qv.at[at], q_sem.at[c])

    small_inputs = [
        pltpu.make_async_copy(src, dst, in_sem.at[n])
        for n, (src, dst) in enumerate((
            (models_hbm, models_ref), (first_hbm, first_ref), (second_hbm, second_ref),
            (proj_hbm, proj_ref), (wins_hbm, wins_ref),
        ))
    ]
    for cp in small_inputs:
        cp.start()
    for c in range(chunks):
        qcopy(c).start()

    barrier = pltpu.get_barrier_semaphore()
    for d in range(1, nfeat):
        pl.semaphore_signal(
            barrier, inc=1, device_id=(row, lax.rem(feat + d, nfeat)), device_id_type=MESH
        )
    for d in range(1, nrows):
        pl.semaphore_signal(
            barrier, inc=1, device_id=(lax.rem(row + d, nrows), feat), device_id_type=MESH
        )

    def other(d):
        if chips != 4:
            return lax.rem(chip + d, chips)
        y, x = lax.div(chip, 2), lax.rem(chip, 2)
        return ((y * 2 + 1 - x), ((1 - y) * 2 + x), ((1 - y) * 2 + 1 - x))[d - 1]

    def remote(src, dst, send, recv, to_row, to_feat):
        return pltpu.make_async_remote_copy(
            src_ref=src, dst_ref=dst, send_sem=send, recv_sem=recv,
            device_id=(to_row, to_feat), device_id_type=MESH,
        )

    def push(*args):
        remote(*args).start()

    def arrived(view, recv):
        remote(view, view, recv, recv, partner, feat).wait_recv()

    def all_sent(view, send):
        remote(view, view, send, send, partner, feat).wait_send()

    eye = (
        lax.broadcasted_iota(jnp.int32, (rdim, rdim), 0)
        == lax.broadcasted_iota(jnp.int32, (rdim, rdim), 1)
    ).astype(F32).astype(BF16)
    for cp in small_inputs[:3]:
        cp.wait()
    models3 = jnp.concatenate(split3(models_ref[...]), axis=0)
    models3_t = dot_nt(eye, models3).astype(BF16)

    label = lax.broadcasted_iota(jnp.int32, (nm, SUB), 0)
    for s in range(tokens // SUB):
        at = pl.ds(s * SUB, SUB)
        pick = (
            (label == first_ref[:, at]).astype(F32) - (label == second_ref[:, at]).astype(F32)
        ).astype(BF16)
        pick_v[:, at] = pick
        pick3 = jnp.concatenate([pick, pick, pick], axis=0)
        gap_v[:, at] = jnp.dot(models3_t, pick3, preferred_element_type=F32)

    for cp in small_inputs[3:]:
        cp.wait()
    proj_t = dot_nt(eye, proj_ref[...]).astype(BF16)

    def partial_margins(c):
        qcopy(c).wait()
        for s in range(t // SUB):
            at = pl.ds(c * t + s * SUB, SUB)
            routed = dot_nt(proj_t, qv[at, :])
            routed_v[:, at] = routed
            marg[feat, :, at] = jnp.sum(routed * gap_v[:, at], axis=0, keepdims=True)

    groups = (range(early), range(early, chunks))

    def cut(g):
        return pl.ds(groups[g].start * t, len(groups[g]) * t)

    for g in range(2):
        for c in groups[g]:
            partial_margins(c)
        if g == 0:
            pl.semaphore_wait(barrier, nfeat - 1 + nrows - 1)
        for d in range(1, nfeat):
            view = marg.at[feat, :, cut(g)]
            push(view, view, mg_s, mg_r.at[g], row, lax.rem(feat + d, nfeat))

    def block_of(i):
        if gpb == 1 and chips == 4:
            return other(3 - i) if i < 3 else chip
        return lax.rem(lax.div(chip, gpb) + 1 + i, blocks)

    def block_part(i, g, acc):
        cols = pl.ds(pl.multiple_of(block_of(i) * bw, 128), bw)
        for c in groups[g]:
            at = pl.ds(c * t, t)
            acc = acc + jnp.dot(back_v[:, at], qv[at, cols], preferred_element_type=F32)
        return acc

    loss_row = jnp.zeros((1, t), F32)
    msum = jnp.zeros((nm, 2 * rdim), F32)
    for g in range(2):
        arrived(marg.at[pl.ds(0, nfeat - 1), :, cut(g)], mg_r.at[g])
        for c in groups[g]:
            at = pl.ds(c * t, t)
            margin = marg[0, :, at]
            for z in range(1, nfeat):
                margin = margin + marg[z, :, at]
            sign = 2.0 * wins_ref[:, at].astype(F32) - 1.0
            x = -sign * margin
            loss_row = loss_row + (jnp.maximum(x, 0.0) + jnp.log1p(jnp.exp(-jnp.abs(x))))
            coef = -sign * jax.nn.sigmoid(x) / total_rows
            for s in range(t // SUB):
                sub = pl.ds(c * t + s * SUB, SUB)
                cs = coef[:, s * SUB:(s + 1) * SUB]
                back_v[:, sub] = (cs * gap_v[:, sub]).astype(BF16)
                w = cs * routed_v[:, sub]
                hi = w.astype(BF16)
                lo = (w - hi.astype(F32)).astype(BF16)
                msum = msum + dot_nt(pick_v[:, sub], jnp.concatenate([hi, lo], axis=0))
        if g == 0:
            for i in range(blocks):
                acc_v[i] = block_part(i, 0, jnp.zeros((rdim, bw), F32))

    mbuf[0:nm, :] = msum[:, :rdim] + msum[:, rdim:]
    lsum = loss_row[:, 0:rdim]
    for i in range(1, t // rdim):
        lsum = lsum + loss_row[:, i * rdim:(i + 1) * rdim]
    tail = mbuf.shape[0] - nm
    mbuf[nm:, :] = jnp.where(
        lax.broadcasted_iota(jnp.int32, (tail, rdim), 0) == 0,
        jnp.broadcast_to(lsum, (tail, rdim)), 0.0,
    )
    push(mbuf.at[pl.ds((1 - core) * mh, mh)], mprt, ma_s, ma_r, partner, feat)

    def block_grad(i):
        gblk[i] = block_part(i, 1, acc_v[i]).T
        push(gblk.at[i, pl.ds((1 - core) * half, half)], prt.at[i], pr_s, pr_r.at[i], partner, feat)

    def chip_sum(i):
        arrived(prt.at[i], pr_r.at[i])
        csum[i] = gblk[i, pl.ds(core * half, half), :] + prt[i]
        for j in range(gpb):
            to = block_of(i) * gpb + j
            mine = pl.ds(j * fs, fs)

            def send():
                push(csum.at[i, mine], rbuf.at[chip], rs_s, rs_r, to * 2 + core, feat)

            def keep():
                rbuf[chip] = csum[i, mine, :]

            if gpb > 1:
                pl.when(to != chip)(send)
                pl.when(to == chip)(keep)
            elif i < blocks - 1:
                send()
            else:
                keep()

    for i in range(blocks):
        block_grad(i)
        if i > 0:
            chip_sum(i - 1)
    arrived(mprt, ma_r)
    mrow[chip] = mbuf[pl.ds(core * mh, mh), :] + mprt[...]
    for d in range(chips - 1, 0, -1):
        push(mrow.at[chip], mrow.at[chip], mb_s, mb_r, other(d) * 2 + core, feat)
    chip_sum(blocks - 1)
    arrived(mrow.at[pl.ds(0, chips - 1)], mb_r)
    mr = mrow[0]
    for i in range(1, chips):
        mr = mr + mrow[i]
    mfeat[feat] = mr
    for d in range(1, nfeat):
        push(mfeat.at[feat], mfeat.at[feat], mc_s, mc_r, row, lax.rem(feat + d, nfeat))

    def slice_of(c, k):
        start = lax.div(c, gpb) * bw + k * half + lax.rem(c, gpb) * fs
        return gfull.at[pl.ds(pl.multiple_of(start, 8), fs)]

    arrived(rbuf.at[pl.ds(0, chips - 1)], rs_r)
    own = rbuf[0]
    for i in range(1, chips):
        own = own + rbuf[i]
    mine = slice_of(chip, core)
    mine[...] = own
    for d in range(chips - 1, 0, -1):
        push(mine, mine, ag_s, ag_r.at[chip], other(d) * 2 + core, feat)
    push(mine, mine, fw_s, fw_r, partner, feat)
    square = own * own
    sq = square[0:8]
    for i in range(1, fs // 8):
        sq = sq + square[i * 8:(i + 1) * 8]
    sqf[feat] = sq
    for d in range(1, nfeat):
        push(sqf.at[feat], sqf.at[feat], sf_s, sf_r, row, lax.rem(feat + d, nfeat))

    arrived(sqf.at[pl.ds(0, nfeat - 1)], sf_r)
    sq = sqf[0]
    for i in range(1, nfeat):
        sq = sq + sqf[i]
    sqr[row] = sq
    for d in range(1, nrows):
        push(sqr.at[row], sqr.at[row], sr_s, sr_r, lax.rem(row + d, nrows), feat)

    arrived(mfeat.at[pl.ds(0, nfeat - 1)], mc_r)
    mt = mfeat[0]
    for i in range(1, nfeat):
        mt = mt + mfeat[i]
    mtot[core] = mt
    push(mtot.at[core], mtot.at[core], md_s, md_r, partner, feat)

    for d in range(1, chips):
        view = slice_of(other(d), core)
        arrived(view, ag_r.at[other(d)])
        push(view, view, fw_s, fw_r, partner, feat)

    all_sent(marg.at[pl.ds(0, nfeat - 1)], mg_s)
    all_sent(mprt, ma_s)
    all_sent(mrow.at[pl.ds(0, chips - 1)], mb_s)
    all_sent(mfeat.at[pl.ds(0, nfeat - 1)], mc_s)
    all_sent(prt, pr_s)
    all_sent(rbuf.at[pl.ds(0, chips - 1)], rs_s)
    all_sent(rbuf.at[pl.ds(0, chips - 1)], ag_s)
    all_sent(sqf.at[pl.ds(0, nfeat - 1)], sf_s)

    arrived(mtot.at[1 - core], md_r)
    grad_models = jnp.concatenate([mtot[0], mtot[1]], axis=0)
    loss = jnp.sum(grad_models[nm:]) / total_rows / float(nfeat)
    grad_models = grad_models[:nm]
    model_square = jnp.sum(grad_models * grad_models)
    small_ref[0:nm] = grad_models
    small_ref[nm + 8:] = jnp.full((8, rdim), loss, F32)
    arrived(sqr.at[pl.ds(0, nrows - 1)], sr_r)
    sq = sqr[0]
    for i in range(1, nrows):
        sq = sq + sqr[i]
    total = jnp.sum(sq) + model_square
    entries = jnp.sqrt(jnp.full((8, rdim), float(total_dim * rdim + nm * rdim), F32))
    small_ref[nm:nm + 8] = entries / (jnp.sqrt(jnp.full((8, rdim), total, F32)) + 1e-06)
    arrived(prt, fw_r)
    out_ref[...] = gfull[...]
    all_sent(mtot.at[0], md_s)
    all_sent(sqr.at[pl.ds(0, nrows - 1)], sr_s)
    all_sent(prt, fw_s)


def finish(nm, grad_ref, small_ref, out_ref, um_ref, loss_ref):
    scale = small_ref[nm:nm + 1, :]
    out_ref[...] = scale * grad_ref[...]
    um_ref[...] = scale * small_ref[0:nm, :]
    loss_ref[0, 0] = small_ref[nm + 8, 0]


def body(queries, projection, models, first, second, wins):
    nrows, nfeat = lax.axis_size("rows"), lax.axis_size("feat")
    tokens, dloc = queries.shape
    rdim = projection.shape[1]
    nm = models.shape[0]
    chips = nrows // 2
    fs = dloc // nrows
    bw = max(2 * fs, 128)
    blocks = dloc // bw
    half = bw // 2
    chunks = tokens // 1024
    mh = (nm + 16) // 2
    vmem = pl.BlockSpec(memory_space=pltpu.VMEM)
    hbm = pl.BlockSpec(memory_space=pl.ANY)
    dma = pltpu.SemaphoreType.DMA
    grad, small = pl.pallas_call(
        functools.partial(kernel, nrows, nfeat, chunks, blocks, dloc * nfeat),
        out_shape=(
            jax.ShapeDtypeStruct((dloc, rdim), F32),
            jax.ShapeDtypeStruct((nm + 16, rdim), F32),
        ),
        in_specs=[hbm] * 6,
        out_specs=(vmem, vmem),
        scratch_shapes=[
            pltpu.VMEM((tokens, dloc), BF16),
            pltpu.VMEM((dloc, rdim), BF16),
            pltpu.VMEM((nm, rdim), F32),
            pltpu.VMEM((1, tokens), jnp.int32),
            pltpu.VMEM((1, tokens), jnp.int32),
            pltpu.VMEM((1, tokens), jnp.int32),
            pltpu.VMEM((rdim, tokens), F32),
            pltpu.VMEM((rdim, tokens), F32),
            pltpu.VMEM((rdim, tokens), BF16),
            pltpu.VMEM((nm, tokens), BF16),
            pltpu.VMEM((nfeat, 1, tokens), F32),
            pltpu.VMEM((blocks, rdim, bw), F32),
            pltpu.VMEM((blocks, bw, rdim), F32),
            pltpu.VMEM((blocks, half, rdim), F32),
            pltpu.VMEM((blocks, half, rdim), F32),
            pltpu.VMEM((chips, fs, rdim), F32),
            pltpu.VMEM((dloc, rdim), F32),
            pltpu.VMEM((2 * mh, rdim), F32),
            pltpu.VMEM((mh, rdim), F32),
            pltpu.VMEM((chips, mh, rdim), F32),
            pltpu.VMEM((nfeat, mh, rdim), F32),
            pltpu.VMEM((2, mh, rdim), F32),
            pltpu.VMEM((nfeat, 8, rdim), F32),
            pltpu.VMEM((nrows, 8, rdim), F32),
            dma((chunks,)), dma((5,)),
            dma, dma((2,)),
            dma, dma((blocks,)),
            dma, dma,
            dma, dma((chips,)),
            dma, dma,
            dma, dma,
            dma, dma,
            dma, dma,
            dma, dma,
            dma, dma,
            dma, dma,
        ],
        compiler_params=pltpu.CompilerParams(
            collective_id=0, has_side_effects=True, vmem_limit_bytes=60 << 20
        ),
    )(
        queries, projection, models,
        first.reshape(1, tokens), second.reshape(1, tokens), wins.reshape(1, tokens),
    )
    out, um, loss = pl.pallas_call(
        functools.partial(finish, nm),
        out_shape=(
            jax.ShapeDtypeStruct((dloc, rdim), F32),
            jax.ShapeDtypeStruct((nm, rdim), F32),
            jax.ShapeDtypeStruct((1, 1), F32),
        ),
        in_specs=[vmem, vmem],
        out_specs=(vmem, vmem, pl.BlockSpec(memory_space=pltpu.SMEM)),
        name="finish",
    )(grad, small)
    return out, um, loss[0, 0]


def solution(mesh):
    in_specs = (P("rows", "feat"), P("feat", None), P(), P("rows"), P("rows"), P("rows"))
    out_specs = (P("feat", None), P(), P())
    return jax.shard_map(body, mesh=mesh, in_specs=in_specs, out_specs=out_specs, check_vma=False)
```

time: 38.4 us -> 35.7 us (0.930)
  local copies, waits for them, and re-layouts: 3.24 us -> 0 us
  Pallas kernels: 32.6 us -> 34.9 us
  between operations: 2.38 us -> 0.64 us
    unnamed x2 -> x0, local copies, waits for them, and re-layouts: 3.24 us -> none
    pallas_call x0 -> x1, Pallas kernels: none -> 1.9 us  [body(): pl.pallas_call(functools.partial(finish, nm), out_shape=(jax.ShapeDtypeSt...]
    pallas_call x1, Pallas kernels: 32.6 us -> 33 us  [body(): pl.pallas_call(functools.partial(kernel, nrows, nfeat, chunks, blocks, dl...]
where the time goes in v2:
time: 35.7 us; the launch traced here: 35.6 us
  Pallas kernels  34.9 us (98%)
  between operations  0.64 us (2%)
    pallas_call x1, Pallas kernels, body(): pl.pallas_call(functools.partial(kernel, nrows, nfeat, chunks, blocks, dl...  33 us
    pallas_call x1, Pallas kernels, body(): pl.pallas_call(functools.partial(finish, nm), out_shape=(jax.ShapeDtypeSt...  1.9 us

profile of v2, /device:TPU:0, one launch (start us, length us, event | category | flops | bytes accessed | tf_op | source)
XLA Modules:
  0.0 35.6 jit_solution(14363129388212228315)
XLA Ops:
  0.6 33.0 %shard_map.85 = (f32[1024,128]{1,0:T(8,128)}, f32[80,128]{1,0:T(8,128)}) custom-call(bf16[6144,1024]{1,0:T(8,128)(2,1)} %q_hbm.1, bf16[1024,128]{1,0:T(8,128)(2,1)} %proj_hbm.1, f32[64,128]{1,0:T(8,128)} %models_hbm.1, s32[1,6144]{1,0:T(1,128)} %bitcast.4, s32[1,6144]{1,0:T(1,128)} %bitcast.5, s32[1,6144]{1,0:T(1,128)} %bitcast.6), custom_call_target="tpu_custom_call" | custom-call | tf_op jit(solution)/shard_map/pallas_call | solution.py:332
  33.7 1.9 %finish.1 = (f32[1024,128]{1,0:T(8,128)}, f32[64,128]{1,0:T(8,128)}, f32[1,1]{1,0:T(1,128)}) custom-call(f32[1024,128]{1,0:T(8,128)} %get-tuple-element.8.grad_ref, f32[80,128]{1,0:T(8,128)} %get-tuple-element.9.small_ref), custom_call_target="tpu_custom_call" | custom-call | tf_op jit(solution)/shard_map/finish/pallas_call | solution.py:385

commit v3 on v2

--- a/solution.py
+++ b/solution.py
@@ -46,7 +46,7 @@
     rdim = proj_ref.shape[1]
     nm = models_ref.shape[0]
     t = tokens // chunks
-    early = max(1, chunks * 2 // 3)
+    ngroups = mg_r.shape[0]
     bw = dloc // blocks
     half = bw // 2
     fs = dloc // nrows
@@ -54,9 +54,25 @@
     mh = mbuf.shape[0] // 2
     total_rows = float(tokens * nrows)
 
-    def qcopy(c):
-        at = pl.ds(c * t, t)
-        return pltpu.make_async_copy(q_hbm.at[at], qv.at[at], q_sem.at[c])
+    pieces = q_sem.shape[0]
+    flight = 5
+    piece = tokens // pieces
+    state = {"started": 0, "ready": 0}
+
+    def qcopy(n):
+        at = pl.ds(n * piece, piece)
+        return pltpu.make_async_copy(q_hbm.at[at], qv.at[at], q_sem.at[n])
+
+    def stream_to(count):
+        while state["started"] < min(count, pieces):
+            qcopy(state["started"]).start()
+            state["started"] += 1
+
+    def ready_to(count):
+        while state["ready"] < min(count, pieces):
+            qcopy(state["ready"]).wait()
+            state["ready"] += 1
+            stream_to(state["ready"] + flight)
 
     small_inputs = [
         pltpu.make_async_copy(src, dst, in_sem.at[n])
@@ -67,8 +83,7 @@
     ]
     for cp in small_inputs:
         cp.start()
-    for c in range(chunks):
-        qcopy(c).start()
+    stream_to(flight)
 
     barrier = pltpu.get_barrier_semaphore()
     for d in range(1, nfeat):
@@ -119,25 +134,28 @@
         pick_v[:, at] = pick
         pick3 = jnp.concatenate([pick, pick, pick], axis=0)
         gap_v[:, at] = jnp.dot(models3_t, pick3, preferred_element_type=F32)
+        if s % 6 == 5:
+            ready_to(min(s // 6 + 1, 3))
 
     for cp in small_inputs[3:]:
         cp.wait()
     proj_t = dot_nt(eye, proj_ref[...]).astype(BF16)
 
     def partial_margins(c):
-        qcopy(c).wait()
         for s in range(t // SUB):
+            ready_to(((c * t + (s + 1) * SUB - 1) // piece) + 1)
             at = pl.ds(c * t + s * SUB, SUB)
             routed = dot_nt(proj_t, qv[at, :])
             routed_v[:, at] = routed
             marg[feat, :, at] = jnp.sum(routed * gap_v[:, at], axis=0, keepdims=True)
 
-    groups = (range(early), range(early, chunks))
+    ends = [chunks * (g + 1) // ngroups for g in range(ngroups)]
+    groups = [range(a, b) for a, b in zip([0] + ends[:-1], ends)]
 
     def cut(g):
         return pl.ds(groups[g].start * t, len(groups[g]) * t)
 
-    for g in range(2):
+    for g in range(ngroups):
         for c in groups[g]:
             partial_margins(c)
         if g == 0:
@@ -160,7 +178,7 @@
 
     loss_row = jnp.zeros((1, t), F32)
     msum = jnp.zeros((nm, 2 * rdim), F32)
-    for g in range(2):
+    for g in range(ngroups):
         arrived(marg.at[pl.ds(0, nfeat - 1), :, cut(g)], mg_r.at[g])
         for c in groups[g]:
             at = pl.ds(c * t, t)
@@ -179,9 +197,10 @@
                 hi = w.astype(BF16)
                 lo = (w - hi.astype(F32)).astype(BF16)
                 msum = msum + dot_nt(pick_v[:, sub], jnp.concatenate([hi, lo], axis=0))
-        if g == 0:
+        if g < ngroups - 1:
             for i in range(blocks):
-                acc_v[i] = block_part(i, 0, jnp.zeros((rdim, bw), F32))
+                acc = jnp.zeros((rdim, bw), F32) if g == 0 else acc_v[i]
+                acc_v[i] = block_part(i, g, acc)
 
     mbuf[0:nm, :] = msum[:, :rdim] + msum[:, rdim:]
     lsum = loss_row[:, 0:rdim]
@@ -195,7 +214,7 @@
     push(mbuf.at[pl.ds((1 - core) * mh, mh)], mprt, ma_s, ma_r, partner, feat)
 
     def block_grad(i):
-        gblk[i] = block_part(i, 1, acc_v[i]).T
+        gblk[i] = block_part(i, ngroups - 1, acc_v[i]).T
         push(gblk.at[i, pl.ds((1 - core) * half, half)], prt.at[i], pr_s, pr_r.at[i], partner, feat)
 
     def chip_sum(i):
@@ -219,14 +238,19 @@
             else:
                 keep()
 
+    def models_chip():
+        arrived(mprt, ma_r)
+        mrow[chip] = mbuf[pl.ds(core * mh, mh), :] + mprt[...]
+        for d in range(chips - 1, 0, -1):
+            push(mrow.at[chip], mrow.at[chip], mb_s, mb_r, other(d) * 2 + core, feat)
+
     for i in range(blocks):
         block_grad(i)
-        if i > 0:
-            chip_sum(i - 1)
-    arrived(mprt, ma_r)
-    mrow[chip] = mbuf[pl.ds(core * mh, mh), :] + mprt[...]
-    for d in range(chips - 1, 0, -1):
-        push(mrow.at[chip], mrow.at[chip], mb_s, mb_r, other(d) * 2 + core, feat)
+        if i == min(2, blocks - 1):
+            models_chip()
+        if i >= 2:
+            chip_sum(i - 2)
+    chip_sum(blocks - 2)
     chip_sum(blocks - 1)
     arrived(mrow.at[pl.ds(0, chips - 1)], mb_r)
     mr = mrow[0]
@@ -362,8 +386,8 @@
             pltpu.VMEM((2, mh, rdim), F32),
             pltpu.VMEM((nfeat, 8, rdim), F32),
             pltpu.VMEM((nrows, 8, rdim), F32),
-            dma((chunks,)), dma((5,)),
-            dma, dma((2,)),
+            dma((tokens // 512,)), dma((5,)),
+            dma, dma((3,)),
             dma, dma((blocks,)),
             dma, dma,
             dma, dma((chips,)),

time: 35.7 us -> 33.4 us (0.936)
  Pallas kernels: 34.9 us -> 32.6 us
    pallas_call x1, Pallas kernels: 33 us -> 30.7 us  [body(): pl.pallas_call(functools.partial(kernel, nrows, nfeat, chunks, blocks, dl...]
where the time goes in v3:
time: 33.4 us; the launch traced here: 33.3 us
  Pallas kernels  32.6 us (98%)
  between operations  0.64 us (2%)
    pallas_call x1, Pallas kernels, body(): pl.pallas_call(functools.partial(kernel, nrows, nfeat, chunks, blocks, dl...  30.7 us
    pallas_call x1, Pallas kernels, body(): pl.pallas_call(functools.partial(finish, nm), out_shape=(jax.ShapeDtypeSt...  1.9 us

profile of v3, /device:TPU:0, one launch (start us, length us, event | category | flops | bytes accessed | tf_op | source)
XLA Modules:
  0.0 33.3 jit_solution(18412136622536165607)
XLA Ops:
  0.6 30.7 %shard_map.85 = (f32[1024,128]{1,0:T(8,128)}, f32[80,128]{1,0:T(8,128)}) custom-call(bf16[6144,1024]{1,0:T(8,128)(2,1)} %q_hbm.1, bf16[1024,128]{1,0:T(8,128)(2,1)} %proj_hbm.1, f32[64,128]{1,0:T(8,128)} %models_hbm.1, s32[1,6144]{1,0:T(1,128)} %bitcast.4, s32[1,6144]{1,0:T(1,128)} %bitcast.5, s32[1,6144]{1,0:T(1,128)} %bitcast.6), custom_call_target="tpu_custom_call" | custom-call | tf_op jit(solution)/shard_map/pallas_call | solution.py:356
  31.4 1.9 %finish.1 = (f32[1024,128]{1,0:T(8,128)}, f32[64,128]{1,0:T(8,128)}, f32[1,1]{1,0:T(1,128)}) custom-call(f32[1024,128]{1,0:T(8,128)} %get-tuple-element.8.grad_ref, f32[80,128]{1,0:T(8,128)} %get-tuple-element.9.small_ref), custom_call_target="tpu_custom_call" | custom-call | tf_op jit(solution)/shard_map/finish/pallas_call | solution.py:409

commit v4 on v3

--- a/solution.py
+++ b/solution.py
@@ -400,7 +400,7 @@
             dma, dma,
         ],
         compiler_params=pltpu.CompilerParams(
-            collective_id=0, has_side_effects=True, vmem_limit_bytes=60 << 20
+            collective_id=0, has_side_effects=True, vmem_limit_bytes=56 << 20
         ),
     )(
         queries, projection, models,
@@ -415,6 +415,7 @@
         ),
         in_specs=[vmem, vmem],
         out_specs=(vmem, vmem, pl.BlockSpec(memory_space=pltpu.SMEM)),
+        compiler_params=pltpu.CompilerParams(vmem_limit_bytes=8 << 20),
         name="finish",
     )(grad, small)
     return out, um, loss[0, 0]

time: 33.4 us -> 34.3 us (1.027)
  local copies, waits for them, and re-layouts: 0 us -> 1.81 us
  Pallas kernels: 32.6 us -> 31.6 us
    unnamed x0 -> x4, local copies, waits for them, and re-layouts: none -> 1.81 us
    pallas_call x1, Pallas kernels: 1.9 us -> 0.85 us  [body(): pl.pallas_call(functools.partial(finish, nm), out_shape=(jax.ShapeDtypeSt...]
where the time goes in v4:
time: 34.3 us; the launch traced here: 34 us
  Pallas kernels  31.6 us (92%)
  local copies, waits for them, and re-layouts  1.81 us (5%)
  between operations  0.65 us (2%)
    pallas_call x1, Pallas kernels, body(): pl.pallas_call(functools.partial(kernel, nrows, nfeat, chunks, blocks, dl...  30.7 us
    unnamed x4, local copies, waits for them, and re-layouts  1.81 us
    pallas_call x1, Pallas kernels, body(): pl.pallas_call(functools.partial(finish, nm), out_shape=(jax.ShapeDtypeSt...  0.85 us

profile of v4, /device:TPU:0, one launch (start us, length us, event | category | flops | bytes accessed | tf_op | source)
XLA Modules:
  0.0 34.0 jit_solution(8743691647243058845)
XLA Ops:
  0.6 30.7 %shard_map.85 = (f32[1024,128]{1,0:T(8,128)}, f32[80,128]{1,0:T(8,128)}) custom-call(bf16[6144,1024]{1,0:T(8,128)(2,1)} %q_hbm.1, bf16[1024,128]{1,0:T(8,128)(2,1)} %proj_hbm.1, f32[64,128]{1,0:T(8,128)} %models_hbm.1, s32[1,6144]{1,0:T(1,128)} %bitcast.4, s32[1,6144]{1,0:T(1,128)} %bitcast.5, s32[1,6144]{1,0:T(1,128)} %bitcast.6), custom_call_target="tpu_custom_call" | custom-call | tf_op jit(solution)/shard_map/pallas_call | solution.py:356
  31.4 0.0 copy-start
  31.4 1.0 %copy-done = f32[1024,128]{1,0:T(8,128)S(1)} copy-done((f32[1024,128]{1,0:T(8,128)S(1)}, f32[1024,128]{1,0:T(8,128)}, u32[]{:S(2)}) %copy-start) | copy-done | bytes 524312
  32.4 0.0 copy-start.1
  32.4 0.8 %copy-done.1 = f32[80,128]{1,0:T(8,128)S(1)} copy-done((f32[80,128]{1,0:T(8,128)S(1)}, f32[80,128]{1,0:T(8,128)}, u32[]{:S(2)}) %copy-start.1) | copy-done | bytes 40984
  33.2 0.9 %finish.1 = (f32[1024,128]{1,0:T(8,128)}, f32[64,128]{1,0:T(8,128)}, f32[1,1]{1,0:T(1,128)}) custom-call(f32[1024,128]{1,0:T(8,128)S(1)} %copy-done, f32[80,128]{1,0:T(8,128)S(1)} %copy-done.1), custom_call_target="tpu_custom_call" | custom-call | tf_op jit(solution)/shard_map/finish/pallas_call | solution.py:409
Async XLA Ops:
  31.4 1.0 %copy-start = (f32[1024,128]{1,0:T(8,128)S(1)}, f32[1024,128]{1,0:T(8,128)}, u32[]{:S(2)}) copy-start(f32[1024,128]{1,0:T(8,128)} %get-tuple-element.8.grad_ref) | copy-start | bytes 1572868
  32.4 0.8 %copy-start.1 = (f32[80,128]{1,0:T(8,128)S(1)}, f32[80,128]{1,0:T(8,128)}, u32[]{:S(2)}) copy-start(f32[80,128]{1,0:T(8,128)} %get-tuple-element.9.small_ref) | copy-start | bytes 122884
